TPU v7x, 128 devices: a whole 4x4x4 slice. The times are simulated.
128 devices in a mesh: dp: 16 (over x, y), expert: 8 (over z, core).
Axes of the slice: x: 4, y: 4, z: 4, core: 2. Of those that a mesh axis runs over, the one named last changes fastest.
Arguments:
- layer_input: bfloat16 [16384, 2560], P(('dp', 'expert')), may hold values from -6 to 6
- output_grad: bfloat16 [16384, 2560], P(('dp', 'expert')), may hold values from -6 to 6
- expert_ids: int32 [16384, 2], P(('dp', 'expert')), may hold values from 0 to 7, all different within a row; in each aligned block of 128 rows (0 to 127, 128 to 255, ...) at most 48 rows name the same one
- gate_probs: bfloat16 [16384, 2], P(('dp', 'expert')), may hold values from 0.099609375 to 0.59765625
- gate_weight: float32 [8, 2560, 1536], P('expert', 'dp'), may hold values from -0.125 to 0.125
- up_weight: float32 [8, 2560, 1536], P('expert', 'dp'), may hold values from -0.125 to 0.125
- down_weight: float32 [8, 1536, 2560], P('expert', 'dp'), may hold values from -0.15625 to 0.15625
- gate_moment: float32 [8, 2560, 1536], P('expert', 'dp'), may hold values from -12 to 12
- up_moment: float32 [8, 2560, 1536], P('expert', 'dp'), may hold values from -12 to 12
- down_moment: float32 [8, 1536, 2560], P('expert', 'dp'), may hold values from -12 to 12
- gate_second: float32 [8, 2560, 1536], P('expert', 'dp'), may hold values from 1 to 100
- up_second: float32 [8, 2560, 1536], P('expert', 'dp'), may hold values from 1 to 100
- down_second: float32 [8, 1536, 2560], P('expert', 'dp'), may hold values from 1 to 100
Outputs:
- input_grad: bfloat16 [16384, 2560], P(('dp', 'expert'))
- prob_grad: bfloat16 [16384, 2], P(('dp', 'expert'))
- new_gate_weight: float32 [8, 2560, 1536], P('expert', 'dp')
- new_up_weight: float32 [8, 2560, 1536], P('expert', 'dp')
- new_down_weight: float32 [8, 1536, 2560], P('expert', 'dp')
- new_gate_moment: float32 [8, 2560, 1536], P('expert', 'dp')
- new_up_moment: float32 [8, 2560, 1536], P('expert', 'dp')
- new_down_moment: float32 [8, 1536, 2560], P('expert', 'dp')
- new_gate_second: float32 [8, 2560, 1536], P('expert', 'dp')
- new_up_second: float32 [8, 2560, 1536], P('expert', 'dp')
- new_down_second: float32 [8, 1536, 2560], P('expert', 'dp')
Inputs may be any that keep to these rules, and one draw needn't show every extreme that they name: `expert_ids`: each token names 2 different experts. Among the (token, pick) pairs of one device's 128 tokens, no expert is named more than 48 times, and in every draw some device's tokens name some expert exactly 48 times.
All inputs are finite; a program needn't handle non-finite values.
Results may differ from a plain program's by a relative error of at most 0.025.
Values may be sent and summed in bfloat16 or wider, within the bound.
No kernel may reach another device: no remote copies, remote signals or barrier semaphores. Data moves between devices by JAX's collectives and lax.ppermute only.
A program may use at most 256 MiB of HBM per device.

v0:
```python
import jax
import jax.numpy as jnp
from jax import lax
from jax.sharding import PartitionSpec as P

beta_one = 0.9
beta_two = 0.95
learn_rate = 0.003
decay_rate = 0.1
epsilon = 1e-08
correct_one = 1.0 - 2.6561398887587e-05
correct_two = 1.0 - 0.005920529220333


def slot_tables(flat_ids, expert_count, exp_dev, groups, capacity):
    onehot = (flat_ids[:, None] == jnp.arange(expert_count, dtype=jnp.int32)[None, :]).astype(
        jnp.int32
    )
    before = jnp.cumsum(onehot, axis=0) - onehot
    ranked = jnp.sum(before * onehot, axis=1)
    device = flat_ids // exp_dev
    local = flat_ids % exp_dev
    return (local * groups + device) * capacity + ranked


def adamw(weight, moment, second, grad):
    moment_new = beta_one * moment + (1.0 - beta_one) * grad
    second_new = beta_two * second + (1.0 - beta_two) * grad * grad
    update = moment_new / correct_one / (jnp.sqrt(second_new / correct_two) + epsilon)
    return (weight - learn_rate * (update + decay_rate * weight), moment_new, second_new)


def body(
    layer_input,
    output_grad,
    expert_ids,
    gate_probs,
    gate_weight,
    up_weight,
    down_weight,
    gate_moment,
    up_moment,
    down_moment,
    gate_second,
    up_second,
    down_second,
):
    exp_dev = gate_weight.shape[0]
    hidden_units = gate_weight.shape[2]
    width = layer_input.shape[1]
    groups = lax.axis_size("expert")
    shards = lax.axis_size("dp")
    tok_count, picks = expert_ids.shape
    capacity = 3 * tok_count * picks // (2 * exp_dev * groups)
    slots = exp_dev * groups * capacity
    row_count = groups * capacity
    dest_slot = slot_tables(expert_ids.reshape(-1), exp_dev * groups, exp_dev, groups, capacity)
    owner = (
        jnp.zeros((slots,), jnp.int32)
        .at[dest_slot]
        .set(jnp.arange(tok_count * picks, dtype=jnp.int32) // picks)
    )
    filled = jnp.zeros((slots,), jnp.int32).at[dest_slot].set(1) > 0
    zero_val = jnp.zeros((), jnp.bfloat16)
    send_input = jnp.where(filled[:, None], layer_input[owner], zero_val).reshape(
        exp_dev, groups, capacity, width
    )
    send_grad = jnp.where(filled[:, None], output_grad[owner], zero_val).reshape(
        exp_dev, groups, capacity, width
    )
    send_gate = (
        jnp.zeros((slots,), jnp.bfloat16)
        .at[dest_slot]
        .set(gate_probs.reshape(-1))
        .reshape(exp_dev, groups, capacity)
    )
    w_gate_up_shard = jnp.concatenate((gate_weight, up_weight), axis=2).astype(jnp.bfloat16)
    w_down_shard = down_weight.astype(jnp.bfloat16)
    w_gate_up, w_down = (
        lax.all_gather(w_gate_up_shard, "dp", axis=1, tiled=True),
        lax.all_gather(w_down_shard, "dp", axis=1, tiled=True),
    )
    recv_input, recv_grad, recv_gate = (
        lax.all_to_all(send_input, "expert", split_axis=1, concat_axis=1, tiled=True),
        lax.all_to_all(send_grad, "expert", split_axis=1, concat_axis=1, tiled=True),
        lax.all_to_all(send_gate, "expert", split_axis=1, concat_axis=1, tiled=True),
    )
    x_rows = recv_input.reshape(exp_dev, row_count, width)
    dy_rows = recv_grad.reshape(exp_dev, row_count, width)
    gate_rows = recv_gate.reshape(exp_dev, row_count)
    pre = jnp.einsum("erd,edf->erf", x_rows, w_gate_up, preferred_element_type=jnp.float32)
    gate_pre = pre[:, :, :hidden_units]
    up_pre = pre[:, :, hidden_units:]
    sigmoid_gate = jax.nn.sigmoid(gate_pre)
    silu_gate = gate_pre * sigmoid_gate
    hidden = (silu_gate * up_pre).astype(jnp.bfloat16)
    expert_out = jnp.einsum("erf,efd->erd", hidden, w_down, preferred_element_type=jnp.float32)
    prob_rows = jnp.sum(dy_rows.astype(jnp.float32) * expert_out, axis=2).astype(jnp.bfloat16)
    out_scaled = (gate_rows.astype(jnp.float32)[:, :, None] * dy_rows.astype(jnp.float32)).astype(
        jnp.bfloat16
    )
    down_cols = hidden_units // shards
    model_cols = width // shards
    hidden_grad = jnp.einsum("erd,efd->erf", out_scaled, w_down, preferred_element_type=jnp.float32)
    dsilu = sigmoid_gate * (1.0 + gate_pre * (1.0 - sigmoid_gate))
    pre_grad = jnp.concatenate(
        (hidden_grad * up_pre * dsilu, hidden_grad * silu_gate), axis=2
    ).astype(jnp.bfloat16)
    input_rows = jnp.einsum(
        "erf,edf->erd", pre_grad, w_gate_up, preferred_element_type=jnp.float32
    ).astype(jnp.bfloat16)
    cols = x_rows
    first = jnp.einsum("erc,erf->cef", cols, pre_grad, preferred_element_type=jnp.float32).reshape(
        1 * lax.axis_size("dp"), model_cols * exp_dev * 2 * hidden_units
    )
    cols = hidden
    second = jnp.einsum(
        "erc,erd->ced", cols, out_scaled, preferred_element_type=jnp.float32
    ).reshape(1 * lax.axis_size("dp"), down_cols * exp_dev * width)
    joined = lax.psum_scatter(
        jnp.concatenate((first, second), axis=1).astype(jnp.bfloat16),
        "dp",
        scatter_dimension=0,
        tiled=True,
    ).astype(jnp.float32)
    split_at = model_cols * exp_dev * 2 * hidden_units
    grad_gate_up = joined[0, :split_at].reshape(model_cols, exp_dev, 2 * hidden_units)
    grad_down = joined[0, split_at:].reshape(down_cols, exp_dev, width)
    back_input, back_prob = (
        lax.all_to_all(
            input_rows.reshape(exp_dev, groups, capacity, width),
            "expert",
            split_axis=1,
            concat_axis=1,
            tiled=True,
        ),
        lax.all_to_all(
            prob_rows.reshape(exp_dev, groups, capacity),
            "expert",
            split_axis=1,
            concat_axis=1,
            tiled=True,
        ),
    )
    picked_rows = back_input.reshape(slots, width)[dest_slot].reshape(tok_count, picks, width)
    input_grad = jnp.sum(picked_rows.astype(jnp.float32), axis=1).astype(jnp.bfloat16)
    prob_grad = back_prob.reshape(slots)[dest_slot].reshape(tok_count, picks)
    grad_gate_up = jnp.transpose(grad_gate_up, (1, 0, 2))
    grad_down = jnp.transpose(grad_down, (1, 0, 2))
    new_gate_weight, new_gate_moment, new_gate_second = adamw(
        gate_weight, gate_moment, gate_second, grad_gate_up[:, :, :hidden_units]
    )
    new_up_weight, new_up_moment, new_up_second = adamw(
        up_weight, up_moment, up_second, grad_gate_up[:, :, hidden_units:]
    )
    new_down_weight, new_down_moment, new_down_second = adamw(
        down_weight, down_moment, down_second, grad_down
    )
    return (
        input_grad,
        prob_grad,
        new_gate_weight,
        new_up_weight,
        new_down_weight,
        new_gate_moment,
        new_up_moment,
        new_down_moment,
        new_gate_second,
        new_up_second,
        new_down_second,
    )


def solution(mesh):
    return jax.shard_map(
        body,
        mesh=mesh,
        in_specs=(
            P(("dp", "expert"), None),
            P(("dp", "expert"), None),
            P(("dp", "expert"), None),
            P(("dp", "expert"), None),
            P("expert", "dp", None),
            P("expert", "dp", None),
            P("expert", "dp", None),
            P("expert", "dp", None),
            P("expert", "dp", None),
            P("expert", "dp", None),
            P("expert", "dp", None),
            P("expert", "dp", None),
            P("expert", "dp", None),
        ),
        out_specs=(
            P(("dp", "expert"), None),
            P(("dp", "expert"), None),
            P("expert", "dp", None),
            P("expert", "dp", None),
            P("expert", "dp", None),
            P("expert", "dp", None),
            P("expert", "dp", None),
            P("expert", "dp", None),
            P("expert", "dp", None),
            P("expert", "dp", None),
            P("expert", "dp", None),
        ),
        check_vma=False,
    )
```

profile of v0, /device:TPU:1, one launch (start us, length us, event | category | flops | bytes accessed | tf_op | source)
XLA Modules:
  0.0 654.3 jit_solution(8457311708946021603)
XLA Ops:
  16.7 6.8 %all-to-all-start = ((bf16[1,8,48]{2,0,1:T(2,128)(2,1)}), bf16[1,8,48]{2,0,1:T(2,128)(2,1)S(1)}, u32[]{:S(2)}, u32[]{:S(2)}) async-start(bf16[1,8,48]{2,0,1:T(2,128)(2,1)} %reshape.417), calls=%async_computation | async-start | bytes 8192 | tf_op jit(solution)/shard_map/all_to_all | solution.py:86
  36.3 30.1 %all_to_all.25 = bf16[1,8,48,2560]{3,2,0,1:T(8,128)(2,1)S(1)} all-to-all(bf16[1,8,48,2560]{3,2,0,1:T(8,128)(2,1)} %get-tuple-element.60), channel_id=1, replica_groups=mesh['dp'=16,'expert'=8] {'expert'}, dimensions={1} | all-to-all | bytes 3932160 | tf_op jit(solution)/shard_map/all_to_all | solution.py:85
  66.3 5.1 all-to-all-start.2
  74.1 22.3 %all-to-all-done.2 = bf16[1,8,48,2560]{3,2,0,1:T(8,128)(2,1)} async-done(((bf16[1,8,48,2560]{3,2,0,1:T(8,128)(2,1)}), bf16[1,8,48,2560]{3,2,0,1:T(8,128)(2,1)}, u32[]{:S(2)}, u32[]{:S(2)}) %all-to-all-start.2) | async-done | bytes 1966112 | tf_op jit(solution)/shard_map/all_to_all | solution.py:84
  96.4 23.7 %all-gather.5.cloned.1.call-done = bf16[1,2560,3072]{2,1,0:T(8,128)(2,1)} async-done(((bf16[1,160,3072]{2,1,0:T(8,128)(2,1)}), bf16[1,2560,3072]{2,1,0:T(8,128)(2,1)}) %all-gather.5.cloned.1.call-update) | async-done | bytes 15728656 | tf_op jit(solution)/shard_map/all_gather | solution.py:80
  120.2 11.7 %fusion.13 = f32[1,384,3072]{2,1,0:T(8,128)} fusion(bf16[384,2560]{1,0:T(8,128)(2,1)} %bitcast.12, bf16[1,2560,3072]{2,1,0:T(8,128)(2,1)} %all-gather.5.cloned.1.call-done), kind=kOutput, calls=%fused_computation.21 | convolution fusion | flops 6039797760 | bytes 22413312 | tf_op jit(solution)/shard_map/erd,edf->erf/dot_general | solution.py:91
  131.8 59.3 %all-gather.3.cloned.1.call-done = bf16[1,1536,2560]{2,1,0:T(8,128)(2,1)} async-done(((bf16[1,96,2560]{2,1,0:T(8,128)(2,1)}), bf16[1,1536,2560]{2,1,0:T(8,128)(2,1)}) %all-gather.3.cloned.1.call-update) | async-done | bytes 7864336 | tf_op jit(solution)/shard_map/all_gather | solution.py:81
  191.1 10.8 %fusion.29 = (bf16[384,1536]{1,0:T(8,128)(2,1)S(1)}, bf16[384,1536]{1,0:T(8,128)(2,1)}, bf16[384,1536]{1,0:T(8,128)(2,1)S(1)}) fusion(f32[1,384,3072]{2,1,0:T(8,128)} %fusion.13, bf16[1,1536,2560]{2,1,0:T(8,128)(2,1)} %all-gather.3.cloned.1.call-done, f32[1,384,1,1,1,1,2560]{6,1,5,4,3,2,0:T(8,128)} %bitcast.83, f32[384]{0:T(512)S(1)} %reshape.356), kind=kOutput, calls=%fused_computation.42 | convolution fusion | flops 3030712320 | bytes 20055552 | tf_op jit(solution)/shard_map/erd,efd->erf/dot_general | solution.py:104
  201.9 6.6 %fusion.5 = bf16[1536,1,2560]{0,2,1:T(8,128)(2,1)} fusion(bf16[384,1536]{1,0:T(8,128)(2,1)S(1)} %get-tuple-element.55, f32[1,384,1,1,1,1,2560]{6,1,5,4,3,2,0:T(8,128)S(1)} %bitcast.85, f32[384]{0:T(512)S(1)} %reshape.356), kind=kOutput, calls=%fused_computation.15 | convolution fusion | flops 3025797120 | bytes 12977664 | tf_op jit(solution)/shard_map/erc,erd->ced/dot_general | solution.py:117
  208.6 10.6 %copy.51 = bf16[1536,1,2560]{2,0,1:T(8,128)(2,1)} copy(bf16[1536,1,2560]{0,2,1:T(8,128)(2,1)} %fusion.5) | data formatting | bytes 15728640 | tf_op jit(solution)/shard_map/erc,erd->ced/transpose | solution.py:117
  219.2 7.6 %reshape.355 = bf16[16,245760]{1,0:T(8,128)(2,1)} reshape(bf16[1536,1,2560]{2,0,1:T(8,128)(2,1)} %copy.51) | data formatting | bytes 15728640 | tf_op jit(solution)/shard_map/reshape | solution.py:119
  226.8 13.6 %fusion.4 = bf16[2560,1,3072]{0,2,1:T(8,128)(2,1)} fusion(bf16[384,2560]{1,0:T(8,128)(2,1)} %bitcast.12, bf16[384,1536]{1,0:T(8,128)(2,1)} %get-tuple-element.54, bf16[384,1536]{1,0:T(8,128)(2,1)S(1)} %get-tuple-element.53), kind=kOutput, calls=%fused_computation.13 | convolution fusion | flops 6052380672 | bytes 20054016 | tf_op jit(solution)/shard_map/erc,erf->cef/dot_general | solution.py:113
  240.4 20.7 %copy.50 = bf16[2560,1,3072]{2,0,1:T(8,128)(2,1)} copy(bf16[2560,1,3072]{0,2,1:T(8,128)(2,1)} %fusion.4) | data formatting | bytes 31457280 | tf_op jit(solution)/shard_map/erc,erf->cef/transpose | solution.py:113
  261.1 19.9 %reshape.354 = bf16[16,491520]{1,0:T(8,128)(2,1)} reshape(bf16[2560,1,3072]{2,0,1:T(8,128)(2,1)} %copy.50) | data formatting | bytes 31457280 | tf_op jit(solution)/shard_map/reshape | solution.py:113
  280.9 25.0 %pad_maximum_fusion = bf16[16,737280]{1,0:T(8,128)(2,1)} fusion(bf16[16,245760]{1,0:T(8,128)(2,1)} %reshape.355, bf16[16,491520]{1,0:T(8,128)(2,1)} %reshape.354), kind=kLoop, calls=%fused_computation.7 | loop fusion | flops 47185920 | bytes 47185920 | tf_op jit(solution)/shard_map/concatenate | solution.py:121
  306.0 7.6 %fusion.24 = bf16[384]{0:T(512)(128)(2,1)S(1)} fusion(f32[384,2560]{1,0:T(8,128)} %bitcast.84, bf16[384,1536]{1,0:T(8,128)(2,1)S(1)} %get-tuple-element.55, bf16[1,1536,2560]{2,1,0:T(8,128)(2,1)} %all-gather.3.cloned.1.call-done), kind=kOutput, calls=%fused_computation.36 | convolution fusion | flops 3021864448 | bytes 12976896 | tf_op jit(solution)/shard_map/erf,efd->erd/dot_general | solution.py:97
  314.3 5.1 all-to-all-start.4
  319.4 11.2 %fusion.16 = bf16[384,2560]{1,0:T(8,128)(2,1)} fusion(bf16[1,2560,3072]{2,1,0:T(8,128)(2,1)} %all-gather.5.cloned.1.call-done, bf16[384,1536]{1,0:T(8,128)(2,1)} %get-tuple-element.54, bf16[384,1536]{1,0:T(8,128)(2,1)S(1)} %get-tuple-element.53), kind=kOutput, calls=%fused_computation.22 | convolution fusion | flops 6045499392 | bytes 20054016 | tf_op jit(solution)/shard_map/erf,edf->erd/dot_general | solution.py:109
  330.6 5.4 all-to-all-start.3
  339.4 21.5 %all-to-all-done.3 = bf16[1,8,48,2560]{3,2,0,1:T(8,128)(2,1)S(1)} async-done(((bf16[1,8,48,2560]{3,2,0,1:T(8,128)(2,1)}), bf16[1,8,48,2560]{3,2,0,1:T(8,128)(2,1)S(1)}, u32[]{:S(2)}, u32[]{:S(2)}) %all-to-all-start.3) | async-done | bytes 1966112 | tf_op jit(solution)/shard_map/all_to_all | solution.py:130
  370.9 224.2 %all-reduce.3.cloned.1.call-done = bf16[16,737280]{1,0:T(8,128)(2,1)} async-done(((bf16[16,737280]{1,0:T(8,128)(2,1)}), bf16[16,737280]{1,0:T(8,128)(2,1)}) %all-reduce.3.cloned.1.call-update) | async-done | bytes 23592976
  595.1 7.3 %dynamic-slice_convert_fusion = f32[1,737280]{1,0:T(1,128)S(1)} fusion(bf16[16,737280]{1,0:T(8,128)(2,1)} %all-reduce.3.cloned.1.call-done, u32[]{:T(128)} %bitcast.32), kind=kLoop, calls=%fused_computation.25 | loop fusion | flops 737280 | bytes 4423684 | tf_op jit(solution)/shard_map/convert_element_type | solution.py:125
  602.4 21.6 %slice_reduce_fusion = f32[491520]{0:T(1024)} fusion(f32[1,737280]{1,0:T(1,128)S(1)} %dynamic-slice_convert_fusion), kind=kLoop, calls=%fused_computation.33 | loop fusion | bytes 3932160 | tf_op jit(solution)/shard_map/slice | solution.py:127
  624.0 11.3 %slice_reduce_fusion.1 = f32[245760]{0:T(1024)} fusion(f32[1,737280]{1,0:T(1,128)S(1)} %dynamic-slice_convert_fusion), kind=kLoop, calls=%fused_computation.46 | loop fusion | bytes 1966080 | tf_op jit(solution)/shard_map/slice | solution.py:128
  (86 shorter events, 51.2 us)
Async XLA Ops:
  7.2 19.3 %copy-start = (bf16[128,2560]{1,0:T(8,128)(2,1)S(1)}, bf16[128,2560]{1,0:T(8,128)(2,1)}, u32[]{:S(2)}) copy-start(bf16[128,2560]{1,0:T(8,128)(2,1)} %param.13) | copy-start | bytes 1966084
  7.2 113.0 %all-gather.5.cloned.1.call-start = ((), (), s32[]{:S(2)}) async-start(), calls=%async_computation.6 | async-start | bytes 16711680 | tf_op jit(solution)/shard_map/all_gather | solution.py:80
  8.6 2.5 copy-start.4
  9.9 2.0 copy-start.11
  9.9 3.5 copy-start.12
  11.0 180.1 %all-gather.3.cloned.1.call-start = ((), (), s32[]{:S(2)}) async-start(), calls=%async_computation.5 | async-start | bytes 8355840 | tf_op jit(solution)/shard_map/all_gather | solution.py:81
  16.7 19.6 %all-to-all-start = ((bf16[1,8,48]{2,0,1:T(2,128)(2,1)}), bf16[1,8,48]{2,0,1:T(2,128)(2,1)S(1)}, u32[]{:S(2)}, u32[]{:S(2)}) async-start(bf16[1,8,48]{2,0,1:T(2,128)(2,1)} %reshape.417), calls=%async_computation | async-start | bytes 8192 | tf_op jit(solution)/shard_map/all_to_all | solution.py:86
  26.5 2.6 copy-start.2
  66.3 30.1 %all-to-all-start.2 = ((bf16[1,8,48,2560]{3,2,0,1:T(8,128)(2,1)}), bf16[1,8,48,2560]{3,2,0,1:T(8,128)(2,1)}, u32[]{:S(2)}, u32[]{:S(2)}) async-start(bf16[1,8,48,2560]{3,2,0,1:T(8,128)(2,1)} %get-tuple-element.59), calls=%async_computation.2 | async-start | bytes 3932160 | tf_op jit(solution)/shard_map/all_to_all | solution.py:84
  71.4 523.7 %all-reduce.3.cloned.1.call-start = ((), (), s32[]{:S(2)}) async-start(), calls=%async_computation.7 | async-start | bytes 47185920
  191.1 10.8 %copy-start.3 = (f32[1,8,48,2560]{3,2,0,1:T(8,128)S(1)}, f32[1,8,48,2560]{3,2,0,1:T(8,128)}, u32[]{:S(2)}) copy-start(f32[1,8,48,2560]{3,2,0,1:T(8,128)} %convert_element_type.140) | copy-start | bytes 11796484
  314.3 16.3 %all-to-all-start.4 = ((bf16[1,8,48]{2,0,1:T(2,128)(2,1)}), bf16[1,8,48]{2,0,1:T(2,128)(2,1)S(1)}, u32[]{:S(2)}, u32[]{:S(2)}) async-start(bf16[1,8,48]{2,0,1:T(2,128)(2,1)} %convert_element_type.142), calls=%async_computation.4 | async-start | bytes 8192 | tf_op jit(solution)/shard_map/all_to_all | solution.py:137
  330.6 5.4 copy-start.13
  330.6 30.2 %all-to-all-start.3 = ((bf16[1,8,48,2560]{3,2,0,1:T(8,128)(2,1)}), bf16[1,8,48,2560]{3,2,0,1:T(8,128)(2,1)S(1)}, u32[]{:S(2)}, u32[]{:S(2)}) async-start(bf16[1,8,48,2560]{3,2,0,1:T(8,128)(2,1)} %bitcast.86), calls=%async_computation.3 | async-start | bytes 3932160 | tf_op jit(solution)/shard_map/all_to_all | solution.py:130
  639.2 4.4 copy-start.5
  639.2 4.4 copy-start.6
  639.2 4.4 copy-start.7
  639.2 4.4 copy-start.8
  639.2 4.4 copy-start.9
  639.2 4.7 copy-start.10
  643.9 3.7 copy-start.1
Sparse Core Ops, SparseCore 0:
  11.1 108.9 all-gather.4
  122.9 68.1 all-gather.2
  306.1 288.8 all-reduce.2
where the time goes:
time: 662 us; the launch traced here: 654 us
  waiting for transfers between devices  351 us (53%)
  local copies, waits for them, and re-layouts  119 us (18%)
  matrix products  61.5 us (9%)
  other arithmetic  56.3 us (9%)
  blocking collectives  30.1 us (5%)
  starting transfers between devices  22.6 us (3%)
  between operations  14.2 us (2%)
    unnamed x4, waiting for transfers between devices  224 us
    all_gather x1, waiting for transfers between devices, body(): lax.all_gather(w_down_shard, 'dp', axis=1, tiled=True)  59.3 us
    all_to_all x1, blocking collectives, body(): lax.all_to_all(send_grad, 'expert', split_axis=1, concat_axis=1, tiled=True)  30.1 us
    concatenate x1, other arithmetic, body(): jnp.concatenate((first, second), axis=1).astype(jnp.bfloat16)  25 us
    all_gather x1, waiting for transfers between devices, body(): lax.all_gather(w_gate_up_shard, 'dp', axis=1, tiled=True)  23.7 us
    all_to_all x1, waiting for transfers between devices, body(): lax.all_to_all(send_input, 'expert', split_axis=1, concat_axis=1, tiled=T...  22.3 us
    slice x1, local copies, waits for them, and re-layouts, body(): joined[0, :split_at].reshape(model_cols, exp_dev, 2 * hidden_units)  21.6 us
    all_to_all x1, waiting for transfers between devices, body(): lax.all_to_all(input_rows.reshape(exp_dev, groups, capacity, width), 'exp...  21.5 us
  transfers between devices with their start and end apart: 7, of which 5 were waited for; matrix products, arithmetic and copies ran while one was open for 10% of the time, Pallas kernels for 0%

commit v1 on v0

--- a/solution.py
+++ b/solution.py
@@ -78,7 +78,9 @@
     w_down_shard = down_weight.astype(jnp.bfloat16)
     w_gate_up, w_down = (
         lax.all_gather(w_gate_up_shard, "dp", axis=1, tiled=True),
-        lax.all_gather(w_down_shard, "dp", axis=1, tiled=True),
+        jnp.concatenate(
+            lax.all_to_all(jnp.stack([w_down_shard] * lax.axis_size("dp")), "dp", 0, 0), axis=1
+        ),
     )
     recv_input, recv_grad, recv_gate = (
         lax.all_to_all(send_input, "expert", split_axis=1, concat_axis=1, tiled=True),

time: 662 us -> 735 us (1.11)
  waiting for transfers between devices: 351 us -> 404 us
  starting transfers between devices: 22.6 us -> 34.6 us
    all_to_all x1 -> x2, waiting for transfers between devices: 22.3 us -> 91.9 us  [the longest x1 68.2 us: body(): lax.all_to_all(jnp.stack([w_down_shard] * lax.axis_size('dp')), 'dp', 0, 0)]
    all_gather x1 -> x0, waiting for transfers between devices: 59.3 us -> none  [body(): lax.all_gather(w_down_shard, 'dp', axis=1, tiled=True)]
    all_gather x1, waiting for transfers between devices: 23.7 us -> 63.4 us  [body(): lax.all_gather(w_gate_up_shard, 'dp', axis=1, tiled=True)]
    unnamed x4 -> x3, waiting for transfers between devices: 224 us -> 228 us
where the time goes in v1:
time: 735 us; the launch traced here: 727 us
  waiting for transfers between devices  404 us (55%)
  local copies, waits for them, and re-layouts  125 us (17%)
  matrix products  62.2 us (8%)
  other arithmetic  56.6 us (8%)
  starting transfers between devices  34.6 us (5%)
  blocking collectives  29.9 us (4%)
  between operations  14.5 us (2%)
    unnamed x3, waiting for transfers between devices  228 us
    all_to_all x1, waiting for transfers between devices, body(): lax.all_to_all(jnp.stack([w_down_shard] * lax.axis_size('dp')), 'dp', 0, 0)  68.2 us
    all_gather x1, waiting for transfers between devices, body(): lax.all_gather(w_gate_up_shard, 'dp', axis=1, tiled=True)  63.4 us
    all_to_all x1, blocking collectives, body(): lax.all_to_all(send_input, 'expert', split_axis=1, concat_axis=1, tiled=T...  29.9 us
    concatenate x1, other arithmetic, body(): jnp.concatenate((first, second), axis=1).astype(jnp.bfloat16)  25 us
    all_to_all x1, waiting for transfers between devices, body(): lax.all_to_all(send_grad, 'expert', split_axis=1, concat_axis=1, tiled=True)  23.7 us
    slice x1, local copies, waits for them, and re-layouts, body(): joined[0, :split_at].reshape(model_cols, exp_dev, 2 * hidden_units)  21.6 us
    all_to_all x1, waiting for transfers between devices, body(): lax.all_to_all(input_rows.reshape(exp_dev, groups, capacity, width), 'exp...  21.5 us
  transfers between devices with their start and end apart: 7, of which 5 were waited for; matrix products, arithmetic and copies ran while one was open for 10% of the time, Pallas kernels for 0%

profile of v1, /device:TPU:1, one launch (start us, length us, event | category | flops | bytes accessed | tf_op | source)
XLA Modules:
  0.0 727.4 jit_solution(16315947534851937295)
XLA Ops:
  15.7 6.8 all-to-all-start
  35.9 29.9 %all_to_all.30 = bf16[1,8,48,2560]{3,2,0,1:T(8,128)(2,1)} all-to-all(bf16[1,8,48,2560]{3,2,0,1:T(8,128)(2,1)S(1)} %get-tuple-element.59), channel_id=1, replica_groups=mesh['dp'=16,'expert'=8] {'expert'}, dimensions={1} | all-to-all | bytes 3932160 | tf_op jit(solution)/shard_map/all_to_all | solution.py:86
  71.4 23.7 %all-to-all-done.1 = bf16[1,8,48,2560]{3,2,0,1:T(8,128)(2,1)S(1)} async-done(((bf16[1,8,48,2560]{3,2,0,1:T(8,128)(2,1)}), bf16[1,8,48,2560]{3,2,0,1:T(8,128)(2,1)S(1)}, u32[]{:S(2)}, u32[]{:S(2)}) %all-to-all-start.1) | async-done | bytes 1966112 | tf_op jit(solution)/shard_map/all_to_all | solution.py:87
  98.9 6.8 all-to-all-start.2
  108.4 63.4 %all-gather.2.cloned.1.call-done = bf16[1,2560,3072]{2,1,0:T(8,128)(2,1)} async-done(((bf16[1,160,3072]{2,1,0:T(8,128)(2,1)}), bf16[1,2560,3072]{2,1,0:T(8,128)(2,1)}) %all-gather.2.cloned.1.call-update) | async-done | bytes 15728656 | tf_op jit(solution)/shard_map/all_gather | solution.py:80
  171.8 11.6 %fusion.6 = f32[1,384,3072]{2,1,0:T(8,128)} fusion(bf16[384,2560]{1,0:T(8,128)(2,1)} %bitcast.78, bf16[1,2560,3072]{2,1,0:T(8,128)(2,1)} %all-gather.2.cloned.1.call-done), kind=kOutput, calls=%fused_computation.17 | convolution fusion | flops 6039797760 | bytes 22413312 | tf_op jit(solution)/shard_map/erd,edf->erf/dot_general | solution.py:93
  183.4 68.2 %all-to-all-done.2 = bf16[16,1,96,2560]{3,2,1,0:T(8,128)(2,1)} async-done(((bf16[16,1,96,2560]{3,2,1,0:T(8,128)(2,1)}), bf16[16,1,96,2560]{3,2,1,0:T(8,128)(2,1)}, u32[]{:S(2)}, u32[]{:S(2)}) %all-to-all-start.2) | async-done | bytes 7864352 | tf_op jit(solution)/shard_map/all_to_all | solution.py:82
  251.6 11.2 %fusion.17 = (bf16[384,1536]{1,0:T(8,128)(2,1)}, bf16[384,1536]{1,0:T(8,128)(2,1)}, bf16[384,1536]{1,0:T(8,128)(2,1)S(1)}) fusion(f32[1,384,3072]{2,1,0:T(8,128)} %fusion.6, bf16[1536,2560]{1,0:T(8,128)(2,1)} %bitcast.9, f32[1,384,1,1,1,1,2560]{6,1,5,4,3,2,0:T(8,128)} %bitcast.75, f32[384]{0:T(512)S(1)} %reshape.362), kind=kOutput, calls=%fused_computation.38 | convolution fusion | flops 3030712320 | bytes 20055552 | tf_op jit(solution)/shard_map/erd,efd->erf/dot_general | solution.py:106
  263.9 6.7 fusion.5
  270.5 10.4 %copy.51 = bf16[1536,1,2560]{2,0,1:T(8,128)(2,1)} copy(bf16[1536,1,2560]{0,2,1:T(8,128)(2,1)} %fusion.5) | data formatting | bytes 15728640 | tf_op jit(solution)/shard_map/erc,erd->ced/transpose | solution.py:119
  281.0 7.8 %reshape.361 = bf16[16,245760]{1,0:T(8,128)(2,1)} reshape(bf16[1536,1,2560]{2,0,1:T(8,128)(2,1)} %copy.51) | data formatting | bytes 15728640 | tf_op jit(solution)/shard_map/reshape | solution.py:121
  288.7 13.7 %fusion.4 = bf16[2560,1,3072]{0,2,1:T(8,128)(2,1)} fusion(bf16[384,2560]{1,0:T(8,128)(2,1)S(1)} %bitcast.79, bf16[384,1536]{1,0:T(8,128)(2,1)} %get-tuple-element.54, bf16[384,1536]{1,0:T(8,128)(2,1)} %get-tuple-element.53), kind=kOutput, calls=%fused_computation.13 | convolution fusion | flops 6052380672 | bytes 20054016 | tf_op jit(solution)/shard_map/erc,erf->cef/dot_general | solution.py:115
  302.4 20.7 %copy.50 = bf16[2560,1,3072]{2,0,1:T(8,128)(2,1)} copy(bf16[2560,1,3072]{0,2,1:T(8,128)(2,1)} %fusion.4) | data formatting | bytes 31457280 | tf_op jit(solution)/shard_map/erc,erf->cef/transpose | solution.py:115
  323.1 19.9 %reshape.360 = bf16[16,491520]{1,0:T(8,128)(2,1)} reshape(bf16[2560,1,3072]{2,0,1:T(8,128)(2,1)} %copy.50) | data formatting | bytes 31457280 | tf_op jit(solution)/shard_map/reshape | solution.py:115
  343.0 25.0 %pad_maximum_fusion = bf16[16,737280]{1,0:T(8,128)(2,1)} fusion(bf16[16,245760]{1,0:T(8,128)(2,1)} %reshape.361, bf16[16,491520]{1,0:T(8,128)(2,1)} %reshape.360), kind=kLoop, calls=%fused_computation.7 | loop fusion | flops 47185920 | bytes 47185920 | tf_op jit(solution)/shard_map/concatenate | solution.py:123
  369.3 7.6 %fusion.14 = bf16[384]{0:T(512)(128)(2,1)S(1)} fusion(f32[384,2560]{1,0:T(8,128)} %bitcast.76, bf16[384,1536]{1,0:T(8,128)(2,1)S(1)} %copy-done.15, bf16[1536,2560]{1,0:T(8,128)(2,1)} %bitcast.9), kind=kOutput, calls=%fused_computation.32 | convolution fusion | flops 3021864448 | bytes 12976896 | tf_op jit(solution)/shard_map/erf,efd->erd/dot_general | solution.py:99
  377.6 11.0 %all-to-all-start.5 = ((bf16[1,8,48]{2,0,1:T(2,128)(2,1)}), bf16[1,8,48]{2,0,1:T(2,128)(2,1)S(1)}, u32[]{:S(2)}, u32[]{:S(2)}) async-start(bf16[1,8,48]{2,0,1:T(2,128)(2,1)} %convert_element_type.145), calls=%async_computation.5 | async-start | bytes 8192 | tf_op jit(solution)/shard_map/all_to_all | solution.py:139
  388.6 11.4 %fusion.9 = bf16[384,2560]{1,0:T(8,128)(2,1)} fusion(bf16[1,2560,3072]{2,1,0:T(8,128)(2,1)} %all-gather.2.cloned.1.call-done, bf16[384,1536]{1,0:T(8,128)(2,1)} %get-tuple-element.54, bf16[384,1536]{1,0:T(8,128)(2,1)} %get-tuple-element.53), kind=kOutput, calls=%fused_computation.18 | convolution fusion | flops 6045499392 | bytes 20054016 | tf_op jit(solution)/shard_map/erf,edf->erd/dot_general | solution.py:111
  400.0 5.4 all-to-all-start.4
  408.8 21.5 %all-to-all-done.4 = bf16[1,8,48,2560]{3,2,0,1:T(8,128)(2,1)S(1)} async-done(((bf16[1,8,48,2560]{3,2,0,1:T(8,128)(2,1)}), bf16[1,8,48,2560]{3,2,0,1:T(8,128)(2,1)S(1)}, u32[]{:S(2)}, u32[]{:S(2)}) %all-to-all-start.4) | async-done | bytes 1966112 | tf_op jit(solution)/shard_map/all_to_all | solution.py:132
  440.3 227.6 %all-reduce.3.cloned.1.call-done = bf16[16,737280]{1,0:T(8,128)(2,1)} async-done(((bf16[16,737280]{1,0:T(8,128)(2,1)}), bf16[16,737280]{1,0:T(8,128)(2,1)}) %all-reduce.3.cloned.1.call-update) | async-done | bytes 23592976
  667.9 7.3 %dynamic-slice_convert_fusion = f32[1,737280]{1,0:T(1,128)S(1)} fusion(bf16[16,737280]{1,0:T(8,128)(2,1)} %all-reduce.3.cloned.1.call-done, u32[]{:T(128)} %bitcast.33), kind=kLoop, calls=%fused_computation.21 | loop fusion | flops 737280 | bytes 4423684 | tf_op jit(solution)/shard_map/convert_element_type | solution.py:127
  675.2 21.6 %slice_reduce_fusion = f32[491520]{0:T(1024)} fusion(f32[1,737280]{1,0:T(1,128)S(1)} %dynamic-slice_convert_fusion), kind=kLoop, calls=%fused_computation.29 | loop fusion | bytes 3932160 | tf_op jit(solution)/shard_map/slice | solution.py:129
  696.8 11.3 %slice_reduce_fusion.1 = f32[245760]{0:T(1024)} fusion(f32[1,737280]{1,0:T(1,128)S(1)} %dynamic-slice_convert_fusion), kind=kLoop, calls=%fused_computation.42 | loop fusion | bytes 1966080 | tf_op jit(solution)/shard_map/slice | solution.py:130
  (90 shorter events, 62.5 us)
Async XLA Ops:
  7.2 18.3 %copy-start = (bf16[128,2560]{1,0:T(8,128)(2,1)S(1)}, bf16[128,2560]{1,0:T(8,128)(2,1)}, u32[]{:S(2)}) copy-start(bf16[128,2560]{1,0:T(8,128)(2,1)} %param.13) | copy-start | bytes 1966084
  7.2 164.6 %all-gather.2.cloned.1.call-start = ((), (), s32[]{:S(2)}) async-start(), calls=%async_computation.6 | async-start | bytes 16711680 | tf_op jit(solution)/shard_map/all_gather | solution.py:80
  8.6 2.4 copy-start.11
  8.6 3.9 copy-start.12
  15.7 20.2 %all-to-all-start = ((bf16[1,8,48]{2,0,1:T(2,128)(2,1)}), bf16[1,8,48]{2,0,1:T(2,128)(2,1)S(1)}, u32[]{:S(2)}, u32[]{:S(2)}) async-start(bf16[1,8,48]{2,0,1:T(2,128)(2,1)} %reshape.423), calls=%async_computation | async-start | bytes 8192 | tf_op jit(solution)/shard_map/all_to_all | solution.py:88
  25.5 3.3 copy-start.2
  65.8 29.3 %all-to-all-start.1 = ((bf16[1,8,48,2560]{3,2,0,1:T(8,128)(2,1)}), bf16[1,8,48,2560]{3,2,0,1:T(8,128)(2,1)S(1)}, u32[]{:S(2)}, u32[]{:S(2)}) async-start(bf16[1,8,48,2560]{3,2,0,1:T(8,128)(2,1)} %get-tuple-element.60), calls=%async_computation.1 | async-start | bytes 3932160 | tf_op jit(solution)/shard_map/all_to_all | solution.py:87
  98.9 152.7 %all-to-all-start.2 = ((bf16[16,1,96,2560]{3,2,1,0:T(8,128)(2,1)}), bf16[16,1,96,2560]{3,2,1,0:T(8,128)(2,1)}, u32[]{:S(2)}, u32[]{:S(2)}) async-start(bf16[16,1,96,2560]{3,2,1,0:T(8,128)(2,1)} %stack.2), calls=%async_computation.2 | async-start | bytes 15728640 | tf_op jit(solution)/shard_map/all_to_all | solution.py:82
  105.7 562.1 %all-reduce.3.cloned.1.call-start = ((), (), s32[]{:S(2)}) async-start(), calls=%async_computation.7 | async-start | bytes 47185920
  251.6 12.2 %copy-start.3 = (f32[1,8,48,2560]{3,2,0,1:T(8,128)S(1)}, f32[1,8,48,2560]{3,2,0,1:T(8,128)}, u32[]{:S(2)}) copy-start(f32[1,8,48,2560]{3,2,0,1:T(8,128)} %convert_element_type.143) | copy-start | bytes 11796484
  262.8 1.0 copy-start.14
  281.0 7.8 %copy-start.6 = (bf16[1,8,48,2560]{3,2,0,1:T(8,128)(2,1)S(1)}, bf16[1,8,48,2560]{3,2,0,1:T(8,128)(2,1)}, u32[]{:S(2)}) copy-start(bf16[1,8,48,2560]{3,2,0,1:T(8,128)(2,1)} %all_to_all.30) | copy-start | bytes 5898244
  368.0 1.3 copy-start.15
  377.6 22.4 %all-to-all-start.5 = ((bf16[1,8,48]{2,0,1:T(2,128)(2,1)}), bf16[1,8,48]{2,0,1:T(2,128)(2,1)S(1)}, u32[]{:S(2)}, u32[]{:S(2)}) async-start(bf16[1,8,48]{2,0,1:T(2,128)(2,1)} %convert_element_type.145), calls=%async_computation.5 | async-start | bytes 8192 | tf_op jit(solution)/shard_map/all_to_all | solution.py:139
  400.0 5.4 copy-start.13
  400.0 30.3 %all-to-all-start.4 = ((bf16[1,8,48,2560]{3,2,0,1:T(8,128)(2,1)}), bf16[1,8,48,2560]{3,2,0,1:T(8,128)(2,1)S(1)}, u32[]{:S(2)}, u32[]{:S(2)}) async-start(bf16[1,8,48,2560]{3,2,0,1:T(8,128)(2,1)} %bitcast.80), calls=%async_computation.4 | async-start | bytes 3932160 | tf_op jit(solution)/shard_map/all_to_all | solution.py:132
  712.0 4.4 copy-start.4
  712.0 4.4 copy-start.5
  712.0 4.4 copy-start.7
  712.0 4.4 copy-start.8
  712.0 4.4 copy-start.9
  712.0 4.7 copy-start.10
  716.7 3.7 copy-start.1
Sparse Core Ops, SparseCore 0:
  11.0 160.6 all-gather.1
  368.1 299.6 all-reduce.2
